TPU v7x, 128 devices: a whole 4x4x4 slice. The times are simulated.
128 devices in a mesh: ctx: 64 (over y_hi, x, z, core), ch: 2 (over y_lo).
Axes of the slice: x: 4, y: 4 (y_hi: 2, y_lo: 2; y = y_hi * 2 + y_lo), z: 4, core: 2. Of those that a mesh axis runs over, the one named last changes fastest.
Arguments:
- qkv: bfloat16 [3, 32768, 4096], P(None, 'ctx', 'ch'), may hold values from -6 to 6
- short_filter: float32 [3, 3, 4096], P(None, None, 'ch'), may hold values from -3 to 3
- long_filter: bfloat16 [2048, 4096], P(None, 'ch'), may hold values from -0.125 to 0.125
- skip: float32 [4096], P('ch'), may hold values from -1 to 1
- shard_doc: int32 [64], replicated, may hold values from 0 to 15, as said below
- live: int32 [64], replicated, may hold values from 1 to 512
Outputs:
- filtered: bfloat16 [2, 2048, 32768], P(None, 'ctx', 'ch')
Inputs may be any that keep to these rules, and one draw needn't show every extreme that they name: `shard_doc`: documents occupy whole consecutive shards in order; each document spans 1 to 16 shards and one spans exactly 16. Read only for a shard that ends a document; its tokens at offsets from live on are padding.
All inputs are finite; a program needn't handle non-finite values.
Results may differ from a plain program's by a relative error of at most 0.012.
Values may be sent and summed in bfloat16 or wider, within the bound.
A program may use at most 256 MiB of HBM per device.

v0:
```python
import functools

import jax
import jax.numpy as jnp
from jax import lax
from jax.experimental import pallas as pl
from jax.experimental.pallas import tpu as pltpu
from jax.sharding import PartitionSpec as P

MESH = pl.DeviceIdType.MESH
LANES = 128
TOK = 512
BLOCKS = TOK // LANES
RING = 32
CHUNKS = 4
HALF = 8
WIDTH = 2 * HALF
SPAN = 16
ROWS = RING * BLOCKS
LAGS = SPAN + 1
TAIL = SPAN // BLOCKS


def bordered(x, above, taps):
    place = lax.broadcasted_iota(jnp.int32, x.shape, 0)
    one = jnp.where(place == 0, above[1:2], pltpu.roll(x, 1, 0))
    two = jnp.where(place == 0, above[0:1], jnp.where(place == 1, above[1:2], pltpu.roll(x, 2, 0)))
    return taps[0:1] * x + taps[1:2] * one + taps[2:3] * two


def gate_kernel(lo_ref, hi_ref, above_lo, above_hi, taps_lo, taps_hi, keep_ref, gated_ref, query_ref):
    keep = keep_ref[...]
    flat = []
    for ref, above, taps in ((lo_ref, above_lo, taps_lo), (hi_ref, above_hi, taps_hi)):
        parts = [
            bordered(ref[a].astype(jnp.float32), above[a].astype(jnp.float32), taps[a])
            for a in range(3)
        ]
        query = parts[0].astype(jnp.bfloat16).astype(jnp.float32) * keep
        gated = parts[1] * parts[2] * keep
        flat.append((gated, query))
    for which, out_ref in enumerate((gated_ref, query_ref)):
        for block in range(BLOCKS):
            rows = slice(block * LANES, (block + 1) * LANES)
            first = flat[0][which][rows].T
            second = flat[1][which][rows].T
            for peer in range(4):
                for chunk in range(CHUNKS):
                    at = peer * 32 + chunk * HALF
                    both = jnp.concatenate([first[at : at + HALF], second[at : at + HALF]], axis=0)
                    out_ref[chunk, peer, block] = both.astype(jnp.bfloat16)


def gate_call(qkv, above, taps, keep):
    width = qkv.shape[2]
    steps = width // (2 * LANES)
    sent = jax.ShapeDtypeStruct((CHUNKS, RING, BLOCKS, WIDTH, LANES), jnp.bfloat16)
    out_spec = pl.BlockSpec((CHUNKS, 4, BLOCKS, WIDTH, LANES), lambda i: (0, i, 0, 0, 0))
    lo = lambda i: (0, 0, i)
    hi = lambda i: (0, 0, i + steps)
    return pl.pallas_call(
        gate_kernel,
        grid=(steps,),
        in_specs=[
            pl.BlockSpec((3, TOK, LANES), lo),
            pl.BlockSpec((3, TOK, LANES), hi),
            pl.BlockSpec((3, 2, LANES), lo),
            pl.BlockSpec((3, 2, LANES), hi),
            pl.BlockSpec((3, 3, LANES), lo),
            pl.BlockSpec((3, 3, LANES), hi),
            pl.BlockSpec((TOK, LANES), lambda i: (0, 0)),
        ],
        out_specs=[out_spec, out_spec],
        out_shape=[sent, sent],
        compiler_params=pltpu.CompilerParams(vmem_limit_bytes=40 * 2**20),
    )(qkv, qkv, above, above, taps, taps, keep)


def displacements():
    groups = [
        [(1, 0), (0, 1), (-1, 0), (0, -1)],
        [(1, 1), (-1, -1)],
        [(1, -1), (-1, 1)],
        [(2, 0), (0, 2)],
        [(2, 1), (1, 2), (2, -1), (-1, 2)],
        [(2, 2)],
    ]
    order = [(dx, dz, core) for core in (0, 1) for group in groups for dx, dz in group]
    return [(0, 0, 1)] + order


def fill_toeplitz(taps_ref, toep_ref, channel, slot):
    taps = taps_ref[channel]
    row = lax.broadcasted_iota(jnp.int32, (LANES, LANES), 0)
    col = lax.broadcasted_iota(jnp.int32, (LANES, LANES), 1)
    causal = col >= row
    older = jnp.zeros((LANES, LANES), jnp.bfloat16)
    for lag in range(LAGS):
        newer = jnp.zeros((LANES, LANES), jnp.bfloat16)
        if lag < SPAN:
            spread = jnp.broadcast_to(taps[lag : lag + 1], (LANES, LANES))
            newer = pltpu.roll(spread, 0, 1, stride=1, stride_axis=0).astype(jnp.bfloat16)
        toep_ref[slot, lag * LANES : (lag + 1) * LANES] = jnp.where(causal, newer, older)
        older = newer


def convolve(wide_ref, toep_ref, mask_ref, total_ref, channel, slot):
    tiles = {
        u: wide_ref[pl.ds((SPAN + u) * WIDTH + channel, 16, stride=8 * WIDTH), :].astype(jnp.bfloat16)
        for u in range(-SPAN, 8)
    }
    columns = [
        jnp.concatenate([tiles[p - lag] for p in range(8)], axis=0) * mask_ref[lag]
        for lag in range(LAGS)
    ]
    left = jnp.concatenate(columns, axis=1)
    total = jnp.dot(left, toep_ref[slot], preferred_element_type=jnp.float32)
    for p in range(8):
        total_ref[pl.ds(p * WIDTH + channel, 16, stride=8 * WIDTH), :] = total[p * 16 : (p + 1) * 16]


def exchange_kernel(
    gated_ref, query_ref, taps_ref, skip_ref, mask_ref, out_ref,
    got, edge, wide, total, ready, toep,
    send_sem, recv_sem, edge_send, edge_recv, turn_send, turn_recv,
):
    place = lax.axis_index("ctx")
    group = lax.axis_index("ch")
    half = place // RING
    ring = lax.rem(place, RING)
    x, z, core = ring // 8, lax.rem(ring // 2, 4), lax.rem(ring, 2)
    base = half * RING

    barrier = pltpu.get_barrier_semaphore()

    @pl.loop(1, RING)
    def _(k):
        peer = (base + lax.rem(ring + k, RING), group)
        pl.semaphore_signal(barrier, inc=1, device_id=peer, device_id_type=MESH)

    for other in range(2):
        @pl.when(jnp.logical_not((half == group) & (group == other)))
        def _():
            peer = (group * RING + ring, other)
            pl.semaphore_signal(barrier, inc=1, device_id=peer, device_id_type=MESH)

    @pl.when(half == 1)
    def _():
        pl.semaphore_signal(barrier, inc=1, device_id=(ring, group), device_id_type=MESH)

    expected = RING - 1 + jnp.where(half == group, 1, 2) + jnp.where(half == 0, 1, 0)
    pl.semaphore_wait(barrier, expected)

    sources = (gated_ref, query_ref)

    def send(chunk, kind):
        for dx, dz, dc in displacements():
            to = (lax.rem(x + dx + 4, 4) * 4 + lax.rem(z + dz + 4, 4)) * 2 + lax.rem(core + dc, 2)
            pltpu.make_async_remote_copy(
                src_ref=sources[kind].at[chunk, to],
                dst_ref=got.at[chunk, kind, ring],
                send_sem=send_sem.at[chunk, kind],
                recv_sem=recv_sem.at[chunk, kind],
                device_id=(base + to, group),
                device_id_type=MESH,
            ).start()
        pltpu.make_async_copy(
            sources[kind].at[chunk, ring], got.at[chunk, kind, ring], recv_sem.at[chunk, kind]
        ).start()

    def arrived(chunk, kind):
        pltpu.make_async_copy(
            sources[kind].at[chunk], got.at[chunk, kind], recv_sem.at[chunk, kind]
        ).wait()

    def edge_copy(chunk):
        return pltpu.make_async_remote_copy(
            src_ref=got.at[chunk, 0, pl.ds(RING - TAIL, TAIL)],
            dst_ref=edge.at[chunk],
            send_sem=edge_send.at[chunk],
            recv_sem=edge_recv.at[chunk],
            device_id=(RING + ring, group),
            device_id_type=MESH,
        )

    def turn_copy(chunk, part):
        return pltpu.make_async_remote_copy(
            src_ref=ready.at[chunk, part],
            dst_ref=out_ref.at[group, pl.ds(chunk * HALF, HALF)],
            send_sem=turn_send.at[chunk, part],
            recv_sem=turn_recv.at[0],
            device_id=(part * RING + ring, half),
            device_id_type=MESH,
        )

    for chunk, kind in ((0, 0), (1, 0), (0, 1), (2, 0), (1, 1), (3, 0), (2, 1), (3, 1)):
        send(chunk, kind)

    @pl.loop(0, CHUNKS)
    def _(chunk):
        arrived(chunk, 0)

        @pl.when(half == 0)
        def _():
            edge_copy(chunk).start()
            wide[pl.ds(0, SPAN * WIDTH)] = jnp.zeros((SPAN * WIDTH, LANES), jnp.float32)

        @pl.loop(0, RING)
        def _(shard):
            at = pl.multiple_of((SPAN + shard * BLOCKS) * WIDTH, 8)
            wide[pl.ds(at, BLOCKS * WIDTH)] = (
                got[chunk, 0, shard].reshape(BLOCKS * WIDTH, LANES).astype(jnp.float32)
            )

        @pl.when(half == 1)
        def _():
            edge_copy(chunk).wait_recv()
            for shard in range(TAIL):
                wide[shard * BLOCKS * WIDTH : (shard + 1) * BLOCKS * WIDTH] = (
                    edge[chunk, shard].reshape(BLOCKS * WIDTH, LANES).astype(jnp.float32)
                )

        @pl.loop(0, WIDTH // 4)
        def _(four):
            for i in range(4):
                fill_toeplitz(taps_ref, toep, chunk * WIDTH + four * 4 + i, i)
            for i in range(4):
                convolve(wide, toep, mask_ref, total, four * 4 + i, i)

        arrived(chunk, 1)
        direct = skip_ref[pl.ds(pl.multiple_of(chunk * WIDTH, WIDTH), WIDTH)]

        @pl.loop(0, RING)
        def _(shard):
            for block in range(BLOCKS):
                row = shard * BLOCKS + block
                at = pl.multiple_of(row * WIDTH, WIDTH)
                gated = got[chunk, 0, shard, block].astype(jnp.float32)
                query = got[chunk, 1, shard, block].astype(jnp.float32)
                value = (query * (total[pl.ds(at, WIDTH)] + direct * gated)).astype(jnp.bfloat16)
                to = pl.multiple_of(row * LANES, LANES)
                ready[chunk, 0, :, pl.ds(to, LANES)] = value[:HALF]
                ready[chunk, 1, :, pl.ds(to, LANES)] = value[HALF:]

        for part in range(2):
            stays = (half == group) & (half == part)

            @pl.when(stays)
            def _():
                pltpu.make_async_copy(
                    ready.at[chunk, part],
                    out_ref.at[group, pl.ds(chunk * HALF, HALF)],
                    turn_recv.at[0],
                ).start()

            @pl.when(jnp.logical_not(stays))
            def _():
                turn_copy(chunk, part).start()

    @pl.loop(0, CHUNKS)
    def _(chunk):
        for kind in range(2):
            pltpu.make_async_remote_copy(
                src_ref=sources[kind].at[chunk, pl.ds(0, RING - 1)],
                dst_ref=got.at[chunk, kind, pl.ds(0, RING - 1)],
                send_sem=send_sem.at[chunk, kind],
                recv_sem=recv_sem.at[chunk, kind],
                device_id=(place, group),
                device_id_type=MESH,
            ).wait_send()
        for part in range(2):
            @pl.when(jnp.logical_not((half == group) & (half == part)))
            def _():
                turn_copy(chunk, part).wait_send()

        @pl.when(half == 0)
        def _():
            edge_copy(chunk).wait_send()

    pltpu.make_async_copy(out_ref, out_ref, turn_recv.at[0]).wait()


def exchange_call(gated, query, taps, skip, mask, tokens):
    vmem = pl.BlockSpec(memory_space=pltpu.VMEM)
    hbm = pl.BlockSpec(memory_space=pl.ANY)
    dma = pltpu.SemaphoreType.DMA
    return pl.pallas_call(
        exchange_kernel,
        out_shape=jax.ShapeDtypeStruct((2, CHUNKS * HALF, tokens), jnp.bfloat16),
        in_specs=[hbm, hbm, vmem, vmem, vmem],
        out_specs=hbm,
        scratch_shapes=[
            pltpu.VMEM((CHUNKS, 2, RING, BLOCKS, WIDTH, LANES), jnp.bfloat16),
            pltpu.VMEM((CHUNKS, TAIL, BLOCKS, WIDTH, LANES), jnp.bfloat16),
            pltpu.VMEM(((SPAN + ROWS) * WIDTH, LANES), jnp.float32),
            pltpu.VMEM((ROWS * WIDTH, LANES), jnp.float32),
            pltpu.VMEM((CHUNKS, 2, HALF, tokens), jnp.bfloat16),
            pltpu.VMEM((4, LAGS * LANES, LANES), jnp.bfloat16),
            dma((CHUNKS, 2)),
            dma((CHUNKS, 2)),
            dma((CHUNKS,)),
            dma((CHUNKS,)),
            dma((CHUNKS, 2)),
            dma((1,)),
        ],
        compiler_params=pltpu.CompilerParams(
            collective_id=0, has_side_effects=True, vmem_limit_bytes=48 * 2**20
        ),
    )(gated, query, taps, skip, mask)


def local(qkv, short_filter, long_filter, skip, shard_doc, live):
    shards = lax.axis_size("ctx")
    here = lax.axis_index("ctx")
    half = here // RING
    ring = lax.rem(here, RING)
    spots = jnp.arange(shards, dtype=jnp.int32)
    before = jnp.concatenate([jnp.full((1,), -1, jnp.int32), shard_doc[:-1]])
    after = jnp.concatenate([shard_doc[1:], jnp.full((1,), -1, jnp.int32)])
    mine = spots == here
    joined = jnp.any(mine & (before == shard_doc))
    closing = jnp.any(mine & (after != shard_doc))
    living = jnp.sum(jnp.where(mine, live, 0))

    route = [(i, i + 1) for i in range(shards - 1)]
    above = lax.ppermute(qkv[:, TOK - 2 :, :], "ctx", route)
    above = jnp.where(joined, above, jnp.zeros_like(above))

    offsets = lax.broadcasted_iota(jnp.int32, (TOK, LANES), 0)
    keep = (jnp.logical_not(closing) | (offsets < living)).astype(jnp.float32)
    gated, query = gate_call(qkv, above, short_filter, keep)

    chosen = lax.dynamic_index_in_dim(
        long_filter.reshape(-1, 2, RING, CHUNKS, HALF), ring, axis=2, keepdims=False
    )
    taps = chosen.transpose(2, 1, 3, 0).reshape(CHUNKS * WIDTH, SPAN, LANES).astype(jnp.float32)
    direct = lax.dynamic_index_in_dim(
        skip.reshape(2, RING, CHUNKS, HALF), ring, axis=1, keepdims=False
    )
    direct = direct.transpose(1, 0, 2).reshape(CHUNKS * WIDTH, 1)
    direct = jnp.broadcast_to(direct, (CHUNKS * WIDTH, LANES))

    index = jnp.arange(ROWS, dtype=jnp.int32)
    row = (index % 16) * 8 + index // 16 + half * ROWS
    source = row[None, :] - jnp.arange(LAGS, dtype=jnp.int32)[:, None]
    opens = (before != shard_doc)[None, :] & (spots[None, :] <= spots[:, None])
    first = jnp.max(jnp.where(opens, spots[None, :], 0), axis=1) * BLOCKS
    start = jnp.sum(
        jnp.where((row // BLOCKS)[:, None] == spots[None, :], first[None, :], 0), axis=1
    )
    mask = (source >= start[None, :]).astype(jnp.bfloat16)
    mask = jnp.broadcast_to(mask[:, :, None], (LAGS, ROWS, LANES))
    return exchange_call(gated, query, taps, direct, mask, ROWS * LANES)


def solution(mesh):
    return jax.shard_map(
        local,
        mesh=mesh,
        in_specs=(P(None, "ctx", "ch"), P(None, None, "ch"), P(None, "ch"), P("ch"), P(), P()),
        out_specs=P(None, "ctx", "ch"),
        check_vma=False,
    )
```

profile of v0, /device:TPU:12, one launch (start us, length us, event | category | flops | bytes accessed | tf_op | source)
XLA Modules:
  0.0 113.4 jit_solution(14845377243646548176)
XLA Ops:
  0.0 0.9 slice.10
  0.9 1.9 %collective-permute-start = (bf16[3,2,2048]{2,1,0:T(2,128)(2,1)S(1)}, bf16[3,2,2048]{2,1,0:T(2,128)(2,1)S(1)}, u32[]{:S(2)}, u32[]{:S(2)}) collective-permute-start(bf16[3,2,2048]{2,1,0:T(2,128)(2,1)S(1)} %slice.10), channel_id=1, source_target_pairs={{0,2},{2,4},{4,6},{6,8},{8,10},{10,12},{12,14},{14,16},{16,18},{18... | collective-permute-start | bytes 73736 | tf_op jit(solution)/shard_map/ppermute | solution.py:326
  2.9 0.0 copy-start.4
  2.9 0.0 copy-start.3
  2.9 0.0 copy-start.5
  2.9 0.0 copy-start.2
  2.9 12.4 %copy.12 = bf16[2048,2048]{0,1:T(8,128)(2,1)} copy(bf16[2048,2048]{1,0:T(8,128)(2,1)} %param.8) | data formatting | bytes 16777216 | tf_op args[2]
  15.3 0.0 copy-done.4
  15.3 0.1 fusion.8
  15.4 0.7 and_reduce_fusion
  16.1 0.1 select_reduce_fusion.1
  16.2 0.0 copy-done.3
  16.2 0.2 reshape.111
  16.4 1.0 convert_bitcast_fusion
  18.1 0.0 copy-done.5
  18.1 0.6 select_reduce_fusion.2
  18.7 0.1 select_reduce_fusion
  18.8 0.7 fusion.3
  19.5 0.1 copy.15
  19.6 0.1 broadcast_in_dim.54
  19.7 0.0 collective-permute-done
  19.7 0.6 broadcast_select_fusion.above_lo.above_hi
  20.3 0.1 iota.33.keep_ref
  20.5 0.0 copy-start
  20.5 2.8 %copy-done = bf16[3,512,2048]{2,1,0:T(8,128)(2,1)S(1)} copy-done((bf16[3,512,2048]{2,1,0:T(8,128)(2,1)S(1)}, bf16[3,512,2048]{2,1,0:T(8,128)(2,1)}, u32[]{:S(2)}) %copy-start) | copy-done | bytes 6291480
  23.3 8.0 %shard_map.64 = (bf16[4,32,4,16,128]{4,3,2,1,0:T(8,128)(2,1)S(1)}, bf16[4,32,4,16,128]{4,3,2,1,0:T(8,128)(2,1)S(1)}) custom-call(bf16[3,512,2048]{2,1,0:T(8,128)(2,1)S(1)} %copy-done, bf16[3,512,2048]{2,1,0:T(8,128)(2,1)S(1)} %copy-done, bf16[3,2,2048]{2,1,0:T(2,128)(2,1)S(1)} %broadcast_select_fusion.above_lo.above_hi, ...), custom_call_target="tpu_custom_call" | custom-call | tf_op jit(solution)/shard_map/pallas_call | solution.py:61
  31.3 0.0 copy-start.1
  31.3 1.3 %copy-done.1 = bf16[4,32,4,16,128]{4,3,2,1,0:T(8,128)(2,1)} copy-done((bf16[4,32,4,16,128]{4,3,2,1,0:T(8,128)(2,1)}, bf16[4,32,4,16,128]{4,3,2,1,0:T(8,128)(2,1)S(1)}, u32[]{:S(2)}) %copy-start.1) | copy-done | bytes 2097176
  32.6 0.3 broadcast_in_dim.59.mask_ref
  33.0 0.1 broadcast_in_dim.55.skip_ref
  33.1 79.0 %shard_map.65 = bf16[2,32,16384]{2,1,0:T(8,128)(2,1)S(1)} custom-call(bf16[4,32,4,16,128]{4,3,2,1,0:T(8,128)(2,1)S(1)} %get-tuple-element.7.gated_ref, bf16[4,32,4,16,128]{4,3,2,1,0:T(8,128)(2,1)} %copy-done.1, f32[64,16,128]{2,1,0:T(8,128)S(1)} %bitcast.14, f32[64,128]{1,0:T(8,128)S(1)} %broadcast_in_dim.55.skip_ref, ...), custom_call_target="tpu_custom_call" | custom-call | tf_op jit(solution)/shard_map/pallas_call | solution.py:287
  112.0 1.3 %copy.17 = bf16[2,32,16384]{2,1,0:T(8,128)(2,1)} copy(bf16[2,32,16384]{2,1,0:T(8,128)(2,1)S(1)} %shard_map.65) | data formatting | bytes 4194304
  (7 shorter events, 0.1 us)
Async XLA Ops:
  0.9 18.8 %collective-permute-start = (bf16[3,2,2048]{2,1,0:T(2,128)(2,1)S(1)}, bf16[3,2,2048]{2,1,0:T(2,128)(2,1)S(1)}, u32[]{:S(2)}, u32[]{:S(2)}) collective-permute-start(bf16[3,2,2048]{2,1,0:T(2,128)(2,1)S(1)} %slice.10), channel_id=1, source_target_pairs={{0,2},{2,4},{4,6},{6,8},{8,10},{10,12},{12,14},{14,16},{16,18},{18... | collective-permute-start | bytes 73736 | tf_op jit(solution)/shard_map/ppermute | solution.py:326
  2.9 12.4 %copy-start.4 = (s32[64]{0:T(128)S(1)}, s32[64]{0:T(128)}, u32[]{:S(2)}) copy-start(s32[64]{0:T(128)} %param.10) | copy-start | bytes 772
  2.9 13.3 %copy-start.3 = (f32[2048]{0:T(1024)S(1)}, f32[2048]{0:T(1024)}, u32[]{:S(2)}) copy-start(f32[2048]{0:T(1024)} %param.9) | copy-start | bytes 24580
  2.9 15.2 %copy-start.5 = (s32[64]{0:T(128)S(1)}, s32[64]{0:T(128)}, u32[]{:S(2)}) copy-start(s32[64]{0:T(128)} %param.11) | copy-start | bytes 772
  2.9 17.6 %copy-start.2 = (f32[3,3,2048]{2,1,0:T(4,128)S(1)}, f32[3,3,2048]{2,1,0:T(4,128)}, u32[]{:S(2)}) copy-start(f32[3,3,2048]{2,1,0:T(4,128)} %taps_hi.1) | copy-start | bytes 221188
  20.5 2.8 %copy-start = (bf16[3,512,2048]{2,1,0:T(8,128)(2,1)S(1)}, bf16[3,512,2048]{2,1,0:T(8,128)(2,1)}, u32[]{:S(2)}) copy-start(bf16[3,512,2048]{2,1,0:T(8,128)(2,1)} %hi_ref.1) | copy-start | bytes 18874372
  31.3 1.3 %copy-start.1 = (bf16[4,32,4,16,128]{4,3,2,1,0:T(8,128)(2,1)}, bf16[4,32,4,16,128]{4,3,2,1,0:T(8,128)(2,1)S(1)}, u32[]{:S(2)}) copy-start(bf16[4,32,4,16,128]{4,3,2,1,0:T(8,128)(2,1)S(1)} %get-tuple-element.8.query_ref) | copy-start | bytes 6291460
where the time goes:
time: 115 us; the launch traced here: 113 us
  Pallas kernels  87 us (76%)
  local copies, waits for them, and re-layouts  19.8 us (17%)
  other arithmetic  3.82 us (3%)
  starting transfers between devices  1.92 us (2%)
    pallas_call x1, Pallas kernels, exchange_call(): pl.pallas_call(exchange_kernel, out_shape=jax.ShapeDtypeStruct((2, CHUNKS...  79 us
    unnamed x15, local copies, waits for them, and re-layouts  17.9 us
    pallas_call x1, Pallas kernels, gate_call(): pl.pallas_call(gate_kernel, grid=(steps,), in_specs=[pl.BlockSpec((3, TOK...  8.05 us
  transfers between devices with their start and end apart: 1, of which 0 were waited for; matrix products, arithmetic and copies ran while one was open for 14% of the time, Pallas kernels for 0%

commit v1 on v0

--- a/solution.py
+++ b/solution.py
@@ -1,5 +1,3 @@
-import functools
-
 import jax
 import jax.numpy as jnp
 from jax import lax
@@ -19,6 +17,7 @@
 ROWS = RING * BLOCKS
 LAGS = SPAN + 1
 TAIL = SPAN // BLOCKS
+STEPS = 8
 
 
 def bordered(x, above, taps):
@@ -26,54 +25,6 @@
     one = jnp.where(place == 0, above[1:2], pltpu.roll(x, 1, 0))
     two = jnp.where(place == 0, above[0:1], jnp.where(place == 1, above[1:2], pltpu.roll(x, 2, 0)))
     return taps[0:1] * x + taps[1:2] * one + taps[2:3] * two
-
-
-def gate_kernel(lo_ref, hi_ref, above_lo, above_hi, taps_lo, taps_hi, keep_ref, gated_ref, query_ref):
-    keep = keep_ref[...]
-    flat = []
-    for ref, above, taps in ((lo_ref, above_lo, taps_lo), (hi_ref, above_hi, taps_hi)):
-        parts = [
-            bordered(ref[a].astype(jnp.float32), above[a].astype(jnp.float32), taps[a])
-            for a in range(3)
-        ]
-        query = parts[0].astype(jnp.bfloat16).astype(jnp.float32) * keep
-        gated = parts[1] * parts[2] * keep
-        flat.append((gated, query))
-    for which, out_ref in enumerate((gated_ref, query_ref)):
-        for block in range(BLOCKS):
-            rows = slice(block * LANES, (block + 1) * LANES)
-            first = flat[0][which][rows].T
-            second = flat[1][which][rows].T
-            for peer in range(4):
-                for chunk in range(CHUNKS):
-                    at = peer * 32 + chunk * HALF
-                    both = jnp.concatenate([first[at : at + HALF], second[at : at + HALF]], axis=0)
-                    out_ref[chunk, peer, block] = both.astype(jnp.bfloat16)
-
-
-def gate_call(qkv, above, taps, keep):
-    width = qkv.shape[2]
-    steps = width // (2 * LANES)
-    sent = jax.ShapeDtypeStruct((CHUNKS, RING, BLOCKS, WIDTH, LANES), jnp.bfloat16)
-    out_spec = pl.BlockSpec((CHUNKS, 4, BLOCKS, WIDTH, LANES), lambda i: (0, i, 0, 0, 0))
-    lo = lambda i: (0, 0, i)
-    hi = lambda i: (0, 0, i + steps)
-    return pl.pallas_call(
-        gate_kernel,
-        grid=(steps,),
-        in_specs=[
-            pl.BlockSpec((3, TOK, LANES), lo),
-            pl.BlockSpec((3, TOK, LANES), hi),
-            pl.BlockSpec((3, 2, LANES), lo),
-            pl.BlockSpec((3, 2, LANES), hi),
-            pl.BlockSpec((3, 3, LANES), lo),
-            pl.BlockSpec((3, 3, LANES), hi),
-            pl.BlockSpec((TOK, LANES), lambda i: (0, 0)),
-        ],
-        out_specs=[out_spec, out_spec],
-        out_shape=[sent, sent],
-        compiler_params=pltpu.CompilerParams(vmem_limit_bytes=40 * 2**20),
-    )(qkv, qkv, above, above, taps, taps, keep)
 
 
 def displacements():
@@ -90,7 +41,6 @@
 
 
 def fill_toeplitz(taps_ref, toep_ref, channel, slot):
-    taps = taps_ref[channel]
     row = lax.broadcasted_iota(jnp.int32, (LANES, LANES), 0)
     col = lax.broadcasted_iota(jnp.int32, (LANES, LANES), 1)
     causal = col >= row
@@ -98,7 +48,7 @@
     for lag in range(LAGS):
         newer = jnp.zeros((LANES, LANES), jnp.bfloat16)
         if lag < SPAN:
-            spread = jnp.broadcast_to(taps[lag : lag + 1], (LANES, LANES))
+            spread = jnp.broadcast_to(taps_ref[lag, pl.ds(channel, 1), :], (LANES, LANES))
             newer = pltpu.roll(spread, 0, 1, stride=1, stride_axis=0).astype(jnp.bfloat16)
         toep_ref[slot, lag * LANES : (lag + 1) * LANES] = jnp.where(causal, newer, older)
         older = newer
@@ -119,13 +69,50 @@
         total_ref[pl.ds(p * WIDTH + channel, 16, stride=8 * WIDTH), :] = total[p * 16 : (p + 1) * 16]
 
 
+def fill_mask(doc_ref, mask_ref, half):
+    shape = (ROWS, LANES)
+    index = lax.broadcasted_iota(jnp.int32, shape, 0)
+    row = lax.rem(index, 16) * 8 + index // 16
+    shard = row // BLOCKS + half * RING
+    first = jnp.zeros(shape, jnp.int32)
+    opened = jnp.int32(0)
+    for spot in range(1, 2 * RING):
+        opened = jnp.where(doc_ref[spot] != doc_ref[spot - 1], jnp.int32(spot), opened)
+        first = jnp.where(shard == spot, opened, first)
+    reach = row + half * ROWS - first * BLOCKS
+    for lag in range(LAGS):
+        mask_ref[lag] = jnp.where(reach >= lag, 1.0, 0.0).astype(jnp.bfloat16)
+
+
+def fill_taps(columns, skip_ref, turned, taps_ref, direct_ref, ring):
+    corner = lax.rem(ring, 4) * 32
+
+    for part in range(2):
+        @pl.loop(0, SPAN)
+        def _(lag):
+            at = pl.multiple_of(lag * LANES, LANES)
+            turned[...] = columns[part, pl.ds(at, LANES), :].astype(jnp.float32).T
+            for chunk in range(CHUNKS):
+                to = chunk * WIDTH + part * HALF
+                taps_ref[lag, to : to + HALF] = turned[pl.ds(pl.multiple_of(corner + chunk * HALF, 8), HALF)]
+
+        line = skip_ref[pl.ds(part * 8 + ring // 4, 1), :]
+        turned[...] = jnp.broadcast_to(line, (LANES, LANES)).T
+        for chunk in range(CHUNKS):
+            to = chunk * WIDTH + part * HALF
+            direct_ref[to : to + HALF] = turned[pl.ds(pl.multiple_of(corner + chunk * HALF, 8), HALF)]
+
+
 def exchange_kernel(
-    gated_ref, query_ref, taps_ref, skip_ref, mask_ref, out_ref,
+    doc_ref, live_ref, qkv_ref, short_ref, filter_ref, skip_ref, out_ref,
+    raw, above, gated_ref, query_ref, columns, turned, taps_ref, direct_ref, mask_ref,
     got, edge, wide, total, ready, toep,
+    load_sem, above_send, above_recv, column_sem,
     send_sem, recv_sem, edge_send, edge_recv, turn_send, turn_recv,
 ):
     place = lax.axis_index("ctx")
     group = lax.axis_index("ch")
+    shards = lax.axis_size("ctx")
     half = place // RING
     ring = lax.rem(place, RING)
     x, z, core = ring // 8, lax.rem(ring // 2, 4), lax.rem(ring, 2)
@@ -148,8 +135,53 @@
     def _():
         pl.semaphore_signal(barrier, inc=1, device_id=(ring, group), device_id_type=MESH)
 
+    @pl.when(place > 0)
+    def _():
+        pl.semaphore_signal(barrier, inc=1, device_id=(place - 1, group), device_id_type=MESH)
+
+    def tile_of(step):
+        near = step + 1
+        return lax.rem(x + near // 2, 4) * 2 + lax.rem(z // 2 + near, 2)
+
+    def load(step, slot, part):
+        lane = pl.multiple_of(tile_of(step) * LANES + part * 8 * LANES, LANES)
+        return pltpu.make_async_copy(
+            qkv_ref.at[:, :, pl.ds(lane, LANES)], raw.at[slot, part], load_sem.at[slot, part]
+        )
+
+    def column(part):
+        lane = pl.multiple_of((ring // 4) * LANES + part * 8 * LANES, LANES)
+        return pltpu.make_async_copy(
+            filter_ref.at[:, pl.ds(lane, LANES)], columns.at[part], column_sem.at[part]
+        )
+
+    above_copy = pltpu.make_async_remote_copy(
+        src_ref=qkv_ref.at[:, pl.ds(TOK - 8, 8)],
+        dst_ref=above,
+        send_sem=above_send,
+        recv_sem=above_recv,
+        device_id=(lax.rem(place + 1, shards), group),
+        device_id_type=MESH,
+    )
+
+    for part in range(2):
+        load(0, 0, part).start()
+    for part in range(2):
+        column(part).start()
+
+    @pl.when(place == 0)
+    def _():
+        above[...] = jnp.zeros_like(above)
+
+    fill_mask(doc_ref, mask_ref, half)
+
     expected = RING - 1 + jnp.where(half == group, 1, 2) + jnp.where(half == 0, 1, 0)
+    expected = expected + jnp.where(place < shards - 1, 1, 0)
     pl.semaphore_wait(barrier, expected)
+
+    @pl.when(place < shards - 1)
+    def _():
+        above_copy.start()
 
     sources = (gated_ref, query_ref)
 
@@ -168,6 +200,27 @@
             sources[kind].at[chunk, ring], got.at[chunk, kind, ring], recv_sem.at[chunk, kind]
         ).start()
 
+    def send_tile(tile, chunk, kind):
+        for member in range(4):
+            to = tile * 4 + member
+
+            @pl.when(to == ring)
+            def _():
+                pltpu.make_async_copy(
+                    sources[kind].at[chunk, to], got.at[chunk, kind, to], recv_sem.at[chunk, kind]
+                ).start()
+
+            @pl.when(to != ring)
+            def _():
+                pltpu.make_async_remote_copy(
+                    src_ref=sources[kind].at[chunk, to],
+                    dst_ref=got.at[chunk, kind, ring],
+                    send_sem=send_sem.at[chunk, kind],
+                    recv_sem=recv_sem.at[chunk, kind],
+                    device_id=(base + to, group),
+                    device_id_type=MESH,
+                ).start()
+
     def arrived(chunk, kind):
         pltpu.make_async_copy(
             sources[kind].at[chunk], got.at[chunk, kind], recv_sem.at[chunk, kind]
@@ -193,8 +246,64 @@
             device_id_type=MESH,
         )
 
-    for chunk, kind in ((0, 0), (1, 0), (0, 1), (2, 0), (1, 1), (3, 0), (2, 1), (3, 1)):
+    doc_here = doc_ref[place]
+    joined = (place > 0) & (doc_ref[jnp.maximum(place - 1, 0)] == doc_here)
+    linked = jnp.where(joined, 1.0, 0.0).astype(jnp.float32)
+    closing = (place == shards - 1) | (doc_ref[jnp.minimum(place + 1, shards - 1)] != doc_here)
+    limit = jnp.where(closing, live_ref[place], TOK)
+
+    @pl.when(place > 0)
+    def _():
+        above_copy.wait_recv()
+
+    @pl.loop(0, STEPS)
+    def _(step):
+        slot = lax.rem(step, 2)
+        tile = tile_of(step)
+        keep = jnp.where(
+            lax.broadcasted_iota(jnp.int32, (TOK, LANES), 0) < limit, 1.0, 0.0
+        ).astype(jnp.float32)
+
+        @pl.when(step + 1 < STEPS)
+        def _():
+            for part in range(2):
+                load(step + 1, 1 - slot, part).start()
+
+        gates = []
+        for part in range(2):
+            load(step, slot, part).wait()
+            lane = pl.multiple_of(tile * LANES + part * 8 * LANES, LANES)
+            parts = [
+                bordered(
+                    raw[slot, part, a].astype(jnp.float32),
+                    above[a, :, pl.ds(lane, LANES)].astype(jnp.float32)[6:8] * linked,
+                    short_ref[a, :, pl.ds(lane, LANES)],
+                )
+                for a in range(3)
+            ]
+            query = parts[0].astype(jnp.bfloat16).astype(jnp.float32) * keep
+            gates.append((parts[1] * parts[2] * keep, query))
+        for which in range(2):
+            for block in range(BLOCKS):
+                rows = slice(block * LANES, (block + 1) * LANES)
+                first = gates[0][which][rows].T
+                second = gates[1][which][rows].T
+                for peer in range(4):
+                    for chunk in range(CHUNKS):
+                        at = peer * 32 + chunk * HALF
+                        both = jnp.concatenate(
+                            [first[at : at + HALF], second[at : at + HALF]], axis=0
+                        )
+                        sources[which][chunk, tile * 4 + peer, block] = both.astype(jnp.bfloat16)
+        send_tile(tile, 0, 0)
+        send_tile(tile, 1, 0)
+
+    for chunk, kind in ((0, 1), (2, 0), (1, 1), (3, 0), (2, 1), (3, 1)):
         send(chunk, kind)
+
+    for part in range(2):
+        column(part).wait()
+    fill_taps(columns, skip_ref, turned, taps_ref, direct_ref, ring)
 
     @pl.loop(0, CHUNKS)
     def _(chunk):
@@ -228,7 +337,7 @@
                 convolve(wide, toep, mask_ref, total, four * 4 + i, i)
 
         arrived(chunk, 1)
-        direct = skip_ref[pl.ds(pl.multiple_of(chunk * WIDTH, WIDTH), WIDTH)]
+        direct = direct_ref[pl.ds(pl.multiple_of(chunk * WIDTH, WIDTH), WIDTH)]
 
         @pl.loop(0, RING)
         def _(shard):
@@ -277,25 +386,45 @@
         def _():
             edge_copy(chunk).wait_send()
 
+    @pl.when(place < shards - 1)
+    def _():
+        above_copy.wait_send()
+
     pltpu.make_async_copy(out_ref, out_ref, turn_recv.at[0]).wait()
 
 
-def exchange_call(gated, query, taps, skip, mask, tokens):
+def local(qkv, short_filter, long_filter, skip, shard_doc, live):
     vmem = pl.BlockSpec(memory_space=pltpu.VMEM)
+    smem = pl.BlockSpec(memory_space=pltpu.SMEM)
     hbm = pl.BlockSpec(memory_space=pl.ANY)
     dma = pltpu.SemaphoreType.DMA
+    tokens = ROWS * LANES
+    parcel = (CHUNKS, RING, BLOCKS, WIDTH, LANES)
     return pl.pallas_call(
         exchange_kernel,
         out_shape=jax.ShapeDtypeStruct((2, CHUNKS * HALF, tokens), jnp.bfloat16),
-        in_specs=[hbm, hbm, vmem, vmem, vmem],
+        in_specs=[smem, smem, hbm, vmem, hbm, vmem],
         out_specs=hbm,
         scratch_shapes=[
+            pltpu.VMEM((2, 2, 3, TOK, LANES), jnp.bfloat16),
+            pltpu.VMEM((3, 8, qkv.shape[2]), jnp.bfloat16),
+            pltpu.VMEM(parcel, jnp.bfloat16),
+            pltpu.VMEM(parcel, jnp.bfloat16),
+            pltpu.VMEM((2, SPAN * LANES, LANES), jnp.bfloat16),
+            pltpu.VMEM((LANES, LANES), jnp.float32),
+            pltpu.VMEM((SPAN, CHUNKS * WIDTH, LANES), jnp.float32),
+            pltpu.VMEM((CHUNKS * WIDTH, LANES), jnp.float32),
+            pltpu.VMEM((LAGS, ROWS, LANES), jnp.bfloat16),
             pltpu.VMEM((CHUNKS, 2, RING, BLOCKS, WIDTH, LANES), jnp.bfloat16),
             pltpu.VMEM((CHUNKS, TAIL, BLOCKS, WIDTH, LANES), jnp.bfloat16),
             pltpu.VMEM(((SPAN + ROWS) * WIDTH, LANES), jnp.float32),
             pltpu.VMEM((ROWS * WIDTH, LANES), jnp.float32),
             pltpu.VMEM((CHUNKS, 2, HALF, tokens), jnp.bfloat16),
             pltpu.VMEM((4, LAGS * LANES, LANES), jnp.bfloat16),
+            dma((2, 2)),
+            dma,
+            dma,
+            dma((2,)),
             dma((CHUNKS, 2)),
             dma((CHUNKS, 2)),
             dma((CHUNKS,)),
@@ -304,53 +433,9 @@
             dma((1,)),
         ],
         compiler_params=pltpu.CompilerParams(
-            collective_id=0, has_side_effects=True, vmem_limit_bytes=48 * 2**20
+            collective_id=0, has_side_effects=True, vmem_limit_bytes=56 * 2**20
         ),
-    )(gated, query, taps, skip, mask)
-
-
-def local(qkv, short_filter, long_filter, skip, shard_doc, live):
-    shards = lax.axis_size("ctx")
-    here = lax.axis_index("ctx")
-    half = here // RING
-    ring = lax.rem(here, RING)
-    spots = jnp.arange(shards, dtype=jnp.int32)
-    before = jnp.concatenate([jnp.full((1,), -1, jnp.int32), shard_doc[:-1]])
-    after = jnp.concatenate([shard_doc[1:], jnp.full((1,), -1, jnp.int32)])
-    mine = spots == here
-    joined = jnp.any(mine & (before == shard_doc))
-    closing = jnp.any(mine & (after != shard_doc))
-    living = jnp.sum(jnp.where(mine, live, 0))
-
-    route = [(i, i + 1) for i in range(shards - 1)]
-    above = lax.ppermute(qkv[:, TOK - 2 :, :], "ctx", route)
-    above = jnp.where(joined, above, jnp.zeros_like(above))
-
-    offsets = lax.broadcasted_iota(jnp.int32, (TOK, LANES), 0)
-    keep = (jnp.logical_not(closing) | (offsets < living)).astype(jnp.float32)
-    gated, query = gate_call(qkv, above, short_filter, keep)
-
-    chosen = lax.dynamic_index_in_dim(
-        long_filter.reshape(-1, 2, RING, CHUNKS, HALF), ring, axis=2, keepdims=False
-    )
-    taps = chosen.transpose(2, 1, 3, 0).reshape(CHUNKS * WIDTH, SPAN, LANES).astype(jnp.float32)
-    direct = lax.dynamic_index_in_dim(
-        skip.reshape(2, RING, CHUNKS, HALF), ring, axis=1, keepdims=False
-    )
-    direct = direct.transpose(1, 0, 2).reshape(CHUNKS * WIDTH, 1)
-    direct = jnp.broadcast_to(direct, (CHUNKS * WIDTH, LANES))
-
-    index = jnp.arange(ROWS, dtype=jnp.int32)
-    row = (index % 16) * 8 + index // 16 + half * ROWS
-    source = row[None, :] - jnp.arange(LAGS, dtype=jnp.int32)[:, None]
-    opens = (before != shard_doc)[None, :] & (spots[None, :] <= spots[:, None])
-    first = jnp.max(jnp.where(opens, spots[None, :], 0), axis=1) * BLOCKS
-    start = jnp.sum(
-        jnp.where((row // BLOCKS)[:, None] == spots[None, :], first[None, :], 0), axis=1
-    )
-    mask = (source >= start[None, :]).astype(jnp.bfloat16)
-    mask = jnp.broadcast_to(mask[:, :, None], (LAGS, ROWS, LANES))
-    return exchange_call(gated, query, taps, direct, mask, ROWS * LANES)
+    )(shard_doc, live, qkv, short_filter, long_filter, skip.reshape(-1, LANES))
 
 
 def solution(mesh):

time: 115 us -> 90.8 us (0.79)
  the two profiles are of different devices: /device:TPU:12 before, /device:TPU:45 now
where the time goes in v1:
time: 90.8 us; the launch traced here: 90.5 us
  Pallas kernels  87.5 us (96%)
  local copies, waits for them, and re-layouts  3.05 us (3%)
    pallas_call x1, Pallas kernels, local(): pl.pallas_call(exchange_kernel, out_shape=jax.ShapeDtypeStruct((2, CHUNKS...  87.5 us
    unnamed x1, local copies, waits for them, and re-layouts  3.05 us

profile of v1, /device:TPU:45, one launch (start us, length us, event | category | flops | bytes accessed | tf_op | source)
XLA Modules:
  0.0 90.5 jit_solution(13132443769581324357)
XLA Ops:
  0.0 87.5 %shard_map.64 = bf16[2,32,16384]{2,1,0:T(8,128)(2,1)} custom-call(s32[64]{0:T(128)} %doc_ref.1, s32[64]{0:T(128)} %live_ref.1, bf16[3,512,2048]{2,1,0:T(8,128)(2,1)} %qkv_ref.1, f32[3,3,2048]{2,1,0:T(4,128)} %short_ref.1, bf16[2048,2048]{1,0:T(8,128)(2,1)} %filter_ref.1, f32[16,128]{1,0:T(8,128)} %bitcast.1), custom_call_target="tpu_custom_call" | custom-call | tf_op jit(solution)/shard_map/pallas_call | solution.py:403
  87.5 3.0 %copy.8 = bf16[2,32,16384]{2,1,0:T(8,128)(2,1)} copy(bf16[2,32,16384]{2,1,0:T(8,128)(2,1)} %shard_map.64) | data formatting | bytes 4194304

commit v2 on v1

--- a/solution.py
+++ b/solution.py
@@ -10,14 +10,17 @@
 TOK = 512
 BLOCKS = TOK // LANES
 RING = 32
-CHUNKS = 4
-HALF = 8
+CHUNKS = 8
+HALF = 4
 WIDTH = 2 * HALF
 SPAN = 16
 ROWS = RING * BLOCKS
 LAGS = SPAN + 1
 TAIL = SPAN // BLOCKS
 STEPS = 8
+PIECES = 4
+LEG = 1
+PIECE = ROWS // PIECES
 
 
 def bordered(x, above, taps):
@@ -29,15 +32,13 @@
 
 def displacements():
     groups = [
+        [(1, 1), (-1, -1), (1, -1), (-1, 1)],
+        [(2, 1), (1, 2), (2, -1), (-1, 2)],
         [(1, 0), (0, 1), (-1, 0), (0, -1)],
-        [(1, 1), (-1, -1)],
-        [(1, -1), (-1, 1)],
-        [(2, 0), (0, 2)],
-        [(2, 1), (1, 2), (2, -1), (-1, 2)],
-        [(2, 2)],
+        [(2, 2), (2, 0), (0, 2)],
     ]
     order = [(dx, dz, core) for core in (0, 1) for group in groups for dx, dz in group]
-    return [(0, 0, 1)] + order
+    return order + [(0, 0, 1)]
 
 
 def fill_toeplitz(taps_ref, toep_ref, channel, slot):
@@ -94,21 +95,21 @@
             turned[...] = columns[part, pl.ds(at, LANES), :].astype(jnp.float32).T
             for chunk in range(CHUNKS):
                 to = chunk * WIDTH + part * HALF
-                taps_ref[lag, to : to + HALF] = turned[pl.ds(pl.multiple_of(corner + chunk * HALF, 8), HALF)]
+                taps_ref[lag, to : to + HALF] = turned[pl.ds(pl.multiple_of(corner + chunk // 2 * 8, 8), 8)][chunk % 2 * HALF : chunk % 2 * HALF + HALF]
 
         line = skip_ref[pl.ds(part * 8 + ring // 4, 1), :]
         turned[...] = jnp.broadcast_to(line, (LANES, LANES)).T
         for chunk in range(CHUNKS):
             to = chunk * WIDTH + part * HALF
-            direct_ref[to : to + HALF] = turned[pl.ds(pl.multiple_of(corner + chunk * HALF, 8), HALF)]
+            direct_ref[to : to + HALF] = turned[pl.ds(pl.multiple_of(corner + chunk // 2 * 8, 8), 8)][chunk % 2 * HALF : chunk % 2 * HALF + HALF]
 
 
 def exchange_kernel(
     doc_ref, live_ref, qkv_ref, short_ref, filter_ref, skip_ref, out_ref,
     raw, above, gated_ref, query_ref, columns, turned, taps_ref, direct_ref, mask_ref,
-    got, edge, wide, total, ready, toep,
+    got, edge, wide, total, ready, relay, toep,
     load_sem, above_send, above_recv, column_sem,
-    send_sem, recv_sem, edge_send, edge_recv, turn_send, turn_recv,
+    send_sem, recv_sem, edge_send, edge_recv, turn_send, turn_recv, relay_send, relay_recv,
 ):
     place = lax.axis_index("ctx")
     group = lax.axis_index("ch")
@@ -125,11 +126,9 @@
         peer = (base + lax.rem(ring + k, RING), group)
         pl.semaphore_signal(barrier, inc=1, device_id=peer, device_id_type=MESH)
 
-    for other in range(2):
-        @pl.when(jnp.logical_not((half == group) & (group == other)))
-        def _():
-            peer = (group * RING + ring, other)
-            pl.semaphore_signal(barrier, inc=1, device_id=peer, device_id_type=MESH)
+    for part in range(2):
+        peer = (part * RING + ring, 1 - group)
+        pl.semaphore_signal(barrier, inc=1, device_id=peer, device_id_type=MESH)
 
     @pl.when(half == 1)
     def _():
@@ -175,7 +174,7 @@
 
     fill_mask(doc_ref, mask_ref, half)
 
-    expected = RING - 1 + jnp.where(half == group, 1, 2) + jnp.where(half == 0, 1, 0)
+    expected = RING + 1 + jnp.where(half == 0, 1, 0)
     expected = expected + jnp.where(place < shards - 1, 1, 0)
     pl.semaphore_wait(barrier, expected)
 
@@ -236,15 +235,60 @@
             device_id_type=MESH,
         )
 
-    def turn_copy(chunk, part):
-        return pltpu.make_async_remote_copy(
-            src_ref=ready.at[chunk, part],
-            dst_ref=out_ref.at[group, pl.ds(chunk * HALF, HALF)],
-            send_sem=turn_send.at[chunk, part],
-            recv_sem=turn_recv.at[0],
-            device_id=(part * RING + ring, half),
-            device_id_type=MESH,
-        )
+    corner = half == group
+
+    def span_of(piece, count=1):
+        return pl.ds(piece * PIECE, PIECE * count)
+
+    def turn(chunk, part, piece):
+        span = span_of(piece)
+        source = ready.at[chunk, part, span]
+
+        @pl.when(jnp.logical_not(corner))
+        def _():
+            pltpu.make_async_remote_copy(
+                src_ref=source,
+                dst_ref=out_ref.at[group, chunk, span],
+                send_sem=turn_send.at[chunk, part],
+                recv_sem=turn_recv.at[0],
+                device_id=(part * RING + ring, 1 - group),
+                device_id_type=MESH,
+            ).start()
+
+        @pl.when(corner & (half == part))
+        def _():
+            pltpu.make_async_copy(
+                source, out_ref.at[group, chunk, span], turn_recv.at[0]
+            ).start()
+
+        @pl.when(corner & (half != part))
+        def _():
+            pltpu.make_async_remote_copy(
+                src_ref=source,
+                dst_ref=relay.at[chunk, span],
+                send_sem=turn_send.at[chunk, part],
+                recv_sem=relay_recv.at[chunk, piece // LEG],
+                device_id=(part * RING + ring, 1 - group),
+                device_id_type=MESH,
+            ).start()
+
+    def forward(chunk):
+        @pl.when(corner)
+        def _():
+            for leg in range(PIECES // LEG):
+                span = span_of(leg * LEG, LEG)
+                copy = pltpu.make_async_remote_copy(
+                    src_ref=relay.at[chunk, span],
+                    dst_ref=out_ref.at[1 - group, chunk, span],
+                    send_sem=relay_send.at[chunk],
+                    recv_sem=turn_recv.at[0],
+                    device_id=(half * RING + ring, 1 - group),
+                    device_id_type=MESH,
+                )
+                pltpu.make_async_copy(
+                    ready.at[chunk, 0, span], relay.at[chunk, span], relay_recv.at[chunk, leg]
+                ).wait()
+                copy.start()
 
     doc_here = doc_ref[place]
     joined = (place > 0) & (doc_ref[jnp.maximum(place - 1, 0)] == doc_here)
@@ -298,15 +342,19 @@
         send_tile(tile, 0, 0)
         send_tile(tile, 1, 0)
 
-    for chunk, kind in ((0, 1), (2, 0), (1, 1), (3, 0), (2, 1), (3, 1)):
-        send(chunk, kind)
+    send(0, 1)
+    send(1, 1)
+
+    @pl.loop(2, CHUNKS)
+    def _(chunk):
+        send(chunk, 0)
+        send(chunk, 1)
 
     for part in range(2):
         column(part).wait()
     fill_taps(columns, skip_ref, turned, taps_ref, direct_ref, ring)
 
-    @pl.loop(0, CHUNKS)
-    def _(chunk):
+    def long_conv(chunk):
         arrived(chunk, 0)
 
         @pl.when(half == 0)
@@ -334,37 +382,37 @@
             for i in range(4):
                 fill_toeplitz(taps_ref, toep, chunk * WIDTH + four * 4 + i, i)
             for i in range(4):
-                convolve(wide, toep, mask_ref, total, four * 4 + i, i)
-
+                convolve(wide, toep, mask_ref, total.at[lax.rem(chunk, 2)], four * 4 + i, i)
+
+    def product(chunk):
         arrived(chunk, 1)
         direct = direct_ref[pl.ds(pl.multiple_of(chunk * WIDTH, WIDTH), WIDTH)]
-
-        @pl.loop(0, RING)
-        def _(shard):
-            for block in range(BLOCKS):
-                row = shard * BLOCKS + block
-                at = pl.multiple_of(row * WIDTH, WIDTH)
-                gated = got[chunk, 0, shard, block].astype(jnp.float32)
-                query = got[chunk, 1, shard, block].astype(jnp.float32)
-                value = (query * (total[pl.ds(at, WIDTH)] + direct * gated)).astype(jnp.bfloat16)
-                to = pl.multiple_of(row * LANES, LANES)
-                ready[chunk, 0, :, pl.ds(to, LANES)] = value[:HALF]
-                ready[chunk, 1, :, pl.ds(to, LANES)] = value[HALF:]
-
-        for part in range(2):
-            stays = (half == group) & (half == part)
-
-            @pl.when(stays)
-            def _():
-                pltpu.make_async_copy(
-                    ready.at[chunk, part],
-                    out_ref.at[group, pl.ds(chunk * HALF, HALF)],
-                    turn_recv.at[0],
-                ).start()
-
-            @pl.when(jnp.logical_not(stays))
-            def _():
-                turn_copy(chunk, part).start()
+        for piece in range(PIECES):
+            @pl.loop(0, RING // PIECES)
+            def _(offset):
+                shard = piece * (RING // PIECES) + offset
+                for block in range(BLOCKS):
+                    row = shard * BLOCKS + block
+                    at = pl.multiple_of(row * WIDTH, WIDTH)
+                    gated = got[chunk, 0, shard, block].astype(jnp.float32)
+                    query = got[chunk, 1, shard, block].astype(jnp.float32)
+                    value = query * (total[lax.rem(chunk, 2), pl.ds(at, WIDTH)] + direct * gated)
+                    ready[chunk, 0, row] = value[:HALF].astype(jnp.bfloat16)
+                    ready[chunk, 1, row] = value[HALF:].astype(jnp.bfloat16)
+
+            for part in range(2):
+                turn(chunk, part, piece)
+
+    @pl.loop(0, CHUNKS)
+    def _(chunk):
+        long_conv(chunk)
+        product(chunk)
+
+        @pl.when(chunk > 0)
+        def _():
+            forward(chunk - 1)
+
+    forward(CHUNKS - 1)
 
     @pl.loop(0, CHUNKS)
     def _(chunk):
@@ -377,10 +425,24 @@
                 device_id=(place, group),
                 device_id_type=MESH,
             ).wait_send()
+        def drained(source, sem):
+            pltpu.make_async_remote_copy(
+                src_ref=source,
+                dst_ref=source,
+                send_sem=sem,
+                recv_sem=turn_recv.at[0],
+                device_id=(place, group),
+                device_id_type=MESH,
+            ).wait_send()
+
         for part in range(2):
-            @pl.when(jnp.logical_not((half == group) & (half == part)))
+            @pl.when(jnp.logical_not(corner & (half == part)))
             def _():
-                turn_copy(chunk, part).wait_send()
+                drained(ready.at[chunk, part], turn_send.at[chunk, part])
+
+        @pl.when(corner)
+        def _():
+            drained(relay.at[chunk], relay_send.at[chunk])
 
         @pl.when(half == 0)
         def _():
@@ -398,11 +460,10 @@
     smem = pl.BlockSpec(memory_space=pltpu.SMEM)
     hbm = pl.BlockSpec(memory_space=pl.ANY)
     dma = pltpu.SemaphoreType.DMA
-    tokens = ROWS * LANES
     parcel = (CHUNKS, RING, BLOCKS, WIDTH, LANES)
-    return pl.pallas_call(
+    moved = pl.pallas_call(
         exchange_kernel,
-        out_shape=jax.ShapeDtypeStruct((2, CHUNKS * HALF, tokens), jnp.bfloat16),
+        out_shape=jax.ShapeDtypeStruct((2, CHUNKS, ROWS, HALF, LANES), jnp.bfloat16),
         in_specs=[smem, smem, hbm, vmem, hbm, vmem],
         out_specs=hbm,
         scratch_shapes=[
@@ -418,8 +479,9 @@
             pltpu.VMEM((CHUNKS, 2, RING, BLOCKS, WIDTH, LANES), jnp.bfloat16),
             pltpu.VMEM((CHUNKS, TAIL, BLOCKS, WIDTH, LANES), jnp.bfloat16),
             pltpu.VMEM(((SPAN + ROWS) * WIDTH, LANES), jnp.float32),
-            pltpu.VMEM((ROWS * WIDTH, LANES), jnp.float32),
-            pltpu.VMEM((CHUNKS, 2, HALF, tokens), jnp.bfloat16),
+            pltpu.VMEM((2, ROWS * WIDTH, LANES), jnp.float32),
+            pltpu.VMEM((CHUNKS, 2, ROWS, HALF, LANES), jnp.bfloat16),
+            pltpu.VMEM((CHUNKS, ROWS, HALF, LANES), jnp.bfloat16),
             pltpu.VMEM((4, LAGS * LANES, LANES), jnp.bfloat16),
             dma((2, 2)),
             dma,
@@ -431,11 +493,14 @@
             dma((CHUNKS,)),
             dma((CHUNKS, 2)),
             dma((1,)),
+            dma((CHUNKS,)),
+            dma((CHUNKS, PIECES // LEG)),
         ],
         compiler_params=pltpu.CompilerParams(
-            collective_id=0, has_side_effects=True, vmem_limit_bytes=56 * 2**20
+            collective_id=0, has_side_effects=True, vmem_limit_bytes=60 * 2**20
         ),
     )(shard_doc, live, qkv, short_filter, long_filter, skip.reshape(-1, LANES))
+    return moved.transpose(0, 1, 3, 2, 4).reshape(2, CHUNKS * HALF, ROWS * LANES)
 
 
 def solution(mesh):

time: 90.8 us -> 83.7 us (0.922)
  the two profiles are of different devices: /device:TPU:45 before, /device:TPU:12 now
where the time goes in v2:
time: 83.7 us; the launch traced here: 82.4 us
  Pallas kernels  78 us (93%)
  local copies, waits for them, and re-layouts  4.44 us (5%)
    pallas_call x1, Pallas kernels, local(): pl.pallas_call(exchange_kernel, out_shape=jax.ShapeDtypeStruct((2, CHUNKS...  78 us
    reshape x1, local copies, waits for them, and re-layouts, local(): moved.transpose(0, 1, 3, 2, 4).reshape(2, CHUNKS * HALF, ROWS * LANES)  2.29 us
    transpose x1, local copies, waits for them, and re-layouts, local(): moved.transpose(0, 1, 3, 2, 4).reshape(2, CHUNKS * HALF, ROWS * LANES)  2.15 us

profile of v2, /device:TPU:12, one launch (start us, length us, event | category | flops | bytes accessed | tf_op | source)
XLA Modules:
  0.0 82.4 jit_solution(14964826550593073741)
XLA Ops:
  0.0 78.0 %shard_map.64 = bf16[2,8,128,4,128]{4,3,2,1,0:T(4,128)(2,1)} custom-call(s32[64]{0:T(128)} %doc_ref.1, s32[64]{0:T(128)} %live_ref.1, bf16[3,512,2048]{2,1,0:T(8,128)(2,1)} %qkv_ref.1, f32[3,3,2048]{2,1,0:T(4,128)} %short_ref.1, bf16[2048,2048]{1,0:T(8,128)(2,1)} %filter_ref.1, f32[16,128]{1,0:T(8,128)} %bitcast.5), custom_call_target="tpu_custom_call" | custom-call | tf_op jit(solution)/shard_map/pallas_call | solution.py:464
  78.0 2.1 %copy.7 = bf16[2,8,4,128,128]{4,3,2,1,0:T(8,128)(2,1)S(1)} copy(bf16[2,8,4,128,128]{4,2,3,1,0:T(4,128)(2,1)} %bitcast.4) | data formatting | bytes 4194304 | tf_op jit(solution)/shard_map/transpose | solution.py:503
  80.2 2.3 %reshape.7 = bf16[2,32,16384]{2,1,0:T(8,128)(2,1)} reshape(bf16[2,8,4,128,128]{4,3,2,1,0:T(8,128)(2,1)S(1)} %copy.7) | data formatting | bytes 4194304 | tf_op jit(solution)/shard_map/reshape | solution.py:503

commit v3 on v2

--- a/solution.py
+++ b/solution.py
@@ -18,6 +18,7 @@
 LAGS = SPAN + 1
 TAIL = SPAN // BLOCKS
 STEPS = 8
+AHEAD = 4
 PIECES = 4
 LEG = 1
 PIECE = ROWS // PIECES
@@ -248,7 +249,7 @@
         def _():
             pltpu.make_async_remote_copy(
                 src_ref=source,
-                dst_ref=out_ref.at[group, chunk, span],
+                dst_ref=out_ref.at[group, chunk // 2, span, pl.ds(lax.rem(chunk, 2) * HALF, HALF)],
                 send_sem=turn_send.at[chunk, part],
                 recv_sem=turn_recv.at[0],
                 device_id=(part * RING + ring, 1 - group),
@@ -258,7 +259,7 @@
         @pl.when(corner & (half == part))
         def _():
             pltpu.make_async_copy(
-                source, out_ref.at[group, chunk, span], turn_recv.at[0]
+                source, out_ref.at[group, chunk // 2, span, pl.ds(lax.rem(chunk, 2) * HALF, HALF)], turn_recv.at[0]
             ).start()
 
         @pl.when(corner & (half != part))
@@ -279,7 +280,7 @@
                 span = span_of(leg * LEG, LEG)
                 copy = pltpu.make_async_remote_copy(
                     src_ref=relay.at[chunk, span],
-                    dst_ref=out_ref.at[1 - group, chunk, span],
+                    dst_ref=out_ref.at[1 - group, chunk // 2, span, pl.ds(lax.rem(chunk, 2) * HALF, HALF)],
                     send_sem=relay_send.at[chunk],
                     recv_sem=turn_recv.at[0],
                     device_id=(half * RING + ring, 1 - group),
@@ -295,6 +296,10 @@
     linked = jnp.where(joined, 1.0, 0.0).astype(jnp.float32)
     closing = (place == shards - 1) | (doc_ref[jnp.minimum(place + 1, shards - 1)] != doc_here)
     limit = jnp.where(closing, live_ref[place], TOK)
+
+    for part in range(2):
+        column(part).wait()
+    fill_taps(columns, skip_ref, turned, taps_ref, direct_ref, ring)
 
     @pl.when(place > 0)
     def _():
@@ -345,16 +350,19 @@
     send(0, 1)
     send(1, 1)
 
-    @pl.loop(2, CHUNKS)
+    @pl.loop(2, AHEAD)
     def _(chunk):
         send(chunk, 0)
         send(chunk, 1)
 
-    for part in range(2):
-        column(part).wait()
-    fill_taps(columns, skip_ref, turned, taps_ref, direct_ref, ring)
 
     def long_conv(chunk):
+        @pl.loop(0, WIDTH // 2)
+        def _(two):
+            for i in range(2):
+                channel = two * 2 + i
+                fill_toeplitz(taps_ref, toep, chunk * WIDTH + channel, channel)
+
         arrived(chunk, 0)
 
         @pl.when(half == 0)
@@ -380,9 +388,8 @@
         @pl.loop(0, WIDTH // 4)
         def _(four):
             for i in range(4):
-                fill_toeplitz(taps_ref, toep, chunk * WIDTH + four * 4 + i, i)
-            for i in range(4):
-                convolve(wide, toep, mask_ref, total.at[lax.rem(chunk, 2)], four * 4 + i, i)
+                channel = four * 4 + i
+                convolve(wide, toep, mask_ref, total.at[lax.rem(chunk, 2)], channel, channel)
 
     def product(chunk):
         arrived(chunk, 1)
@@ -405,6 +412,11 @@
 
     @pl.loop(0, CHUNKS)
     def _(chunk):
+        @pl.when(chunk + AHEAD < CHUNKS)
+        def _():
+            send(chunk + AHEAD, 0)
+            send(chunk + AHEAD, 1)
+
         long_conv(chunk)
         product(chunk)
 
@@ -463,7 +475,7 @@
     parcel = (CHUNKS, RING, BLOCKS, WIDTH, LANES)
     moved = pl.pallas_call(
         exchange_kernel,
-        out_shape=jax.ShapeDtypeStruct((2, CHUNKS, ROWS, HALF, LANES), jnp.bfloat16),
+        out_shape=jax.ShapeDtypeStruct((2, CHUNKS // 2, ROWS, WIDTH, LANES), jnp.bfloat16),
         in_specs=[smem, smem, hbm, vmem, hbm, vmem],
         out_specs=hbm,
         scratch_shapes=[
@@ -482,7 +494,7 @@
             pltpu.VMEM((2, ROWS * WIDTH, LANES), jnp.float32),
             pltpu.VMEM((CHUNKS, 2, ROWS, HALF, LANES), jnp.bfloat16),
             pltpu.VMEM((CHUNKS, ROWS, HALF, LANES), jnp.bfloat16),
-            pltpu.VMEM((4, LAGS * LANES, LANES), jnp.bfloat16),
+            pltpu.VMEM((WIDTH, LAGS * LANES, LANES), jnp.bfloat16),
             dma((2, 2)),
             dma,
             dma,

time: 83.7 us -> 81.3 us (0.971); the launches traced: 82.4 us -> 81.1 us
  local copies, waits for them, and re-layouts: 4.44 us -> 3.05 us
    unnamed x0 -> x1, local copies, waits for them, and re-layouts: none -> 3.05 us
    reshape x1 -> x0, local copies, waits for them, and re-layouts: 2.29 us -> none  [local(): moved.transpose(0, 1, 3, 2, 4).reshape(2, CHUNKS * HALF, ROWS * LANES)]
    transpose x1 -> x0, local copies, waits for them, and re-layouts: 2.15 us -> none  [local(): moved.transpose(0, 1, 3, 2, 4).reshape(2, CHUNKS * HALF, ROWS * LANES)]
where the time goes in v3:
time: 81.3 us; the launch traced here: 81.1 us
  Pallas kernels  78.1 us (96%)
  local copies, waits for them, and re-layouts  3.05 us (4%)
    pallas_call x1, Pallas kernels, local(): pl.pallas_call(exchange_kernel, out_shape=jax.ShapeDtypeStruct((2, CHUNKS...  78.1 us
    unnamed x1, local copies, waits for them, and re-layouts  3.05 us

profile of v3, /device:TPU:12, one launch (start us, length us, event | category | flops | bytes accessed | tf_op | source)
XLA Modules:
  0.0 81.1 jit_solution(11583497719568128054)
XLA Ops:
  0.0 78.1 %shard_map.64 = bf16[2,4,128,8,128]{4,3,2,1,0:T(8,128)(2,1)} custom-call(s32[64]{0:T(128)} %doc_ref.1, s32[64]{0:T(128)} %live_ref.1, bf16[3,512,2048]{2,1,0:T(8,128)(2,1)} %qkv_ref.1, f32[3,3,2048]{2,1,0:T(4,128)} %short_ref.1, bf16[2048,2048]{1,0:T(8,128)(2,1)} %filter_ref.1, f32[16,128]{1,0:T(8,128)} %bitcast.5), custom_call_target="tpu_custom_call" | custom-call | tf_op jit(solution)/shard_map/pallas_call | solution.py:476
  78.1 3.0 %copy.8 = bf16[2,32,16384]{2,1,0:T(8,128)(2,1)} copy(bf16[2,32,16384]{2,1,0:T(8,128)(2,1)} %bitcast.4) | data formatting | bytes 4194304

commit v4 on v3

--- a/solution.py
+++ b/solution.py
@@ -385,10 +385,10 @@
                     edge[chunk, shard].reshape(BLOCKS * WIDTH, LANES).astype(jnp.float32)
                 )
 
-        @pl.loop(0, WIDTH // 4)
+        @pl.loop(0, WIDTH // 8)
         def _(four):
-            for i in range(4):
-                channel = four * 4 + i
+            for i in range(8):
+                channel = four * 8 + i
                 convolve(wide, toep, mask_ref, total.at[lax.rem(chunk, 2)], channel, channel)
 
     def product(chunk):

time: 81.3 us -> 81 us (level)
  no operation moved by 1% of the time
where the time goes in v4:
time: 81 us; the launch traced here: 80.8 us
  Pallas kernels  77.8 us (96%)
  local copies, waits for them, and re-layouts  3.05 us (4%)
    pallas_call x1, Pallas kernels, local(): pl.pallas_call(exchange_kernel, out_shape=jax.ShapeDtypeStruct((2, CHUNKS...  77.8 us
    unnamed x1, local copies, waits for them, and re-layouts  3.05 us

profile of v4, /device:TPU:12, one launch (start us, length us, event | category | flops | bytes accessed | tf_op | source)
XLA Modules:
  0.0 80.8 jit_solution(10153045264035319410)
XLA Ops:
  0.0 77.8 %shard_map.64 = bf16[2,4,128,8,128]{4,3,2,1,0:T(8,128)(2,1)} custom-call(s32[64]{0:T(128)} %doc_ref.1, s32[64]{0:T(128)} %live_ref.1, bf16[3,512,2048]{2,1,0:T(8,128)(2,1)} %qkv_ref.1, f32[3,3,2048]{2,1,0:T(4,128)} %short_ref.1, bf16[2048,2048]{1,0:T(8,128)(2,1)} %filter_ref.1, f32[16,128]{1,0:T(8,128)} %bitcast.5), custom_call_target="tpu_custom_call" | custom-call | tf_op jit(solution)/shard_map/pallas_call | solution.py:476
  77.8 3.0 %copy.8 = bf16[2,32,16384]{2,1,0:T(8,128)(2,1)} copy(bf16[2,32,16384]{2,1,0:T(8,128)(2,1)} %bitcast.4) | data formatting | bytes 4194304
